TPU v7x, 256 devices: a whole 4x4x8 slice. The times are simulated.
256 devices in a mesh: dp: 4 (over y), seq: 16 (over z, core), mp: 4 (over x).
Axes of the slice: x: 4, y: 4, z: 8, core: 2. Of those that a mesh axis runs over, the one named last changes fastest.
Arguments:
- q_self: bfloat16 [4, 1024, 4096], P('dp', 'seq', 'mp'), may hold values from -12 to 12
- k_self: bfloat16 [4, 1024, 4096], P('dp', 'seq', 'mp'), may hold values from -3 to 3
- v_self: bfloat16 [4, 1024, 4096], P('dp', 'seq', 'mp'), may hold values from -0.75 to 0.75
- out_grad_self: bfloat16 [4, 1024, 4096], P('dp', 'seq', 'mp'), may hold values from -6 to 6
- q_cross: bfloat16 [4, 1024, 4096], P('dp', 'seq', 'mp'), may hold values from -12 to 12
- k_cross: bfloat16 [4, 2048, 4096], P('dp', 'seq', 'mp'), may hold values from -3 to 3
- v_cross: bfloat16 [4, 2048, 4096], P('dp', 'seq', 'mp'), may hold values from -0.75 to 0.75
- out_grad_cross: bfloat16 [4, 1024, 4096], P('dp', 'seq', 'mp'), may hold values from -8 to 8
- dec_lengths: int32 [4, 16], P('dp'), may hold values from 1 to 640, as said below
- enc_lengths: int32 [4, 16], P('dp'), may hold values from 1 to 1280, as said below
- rel_bias: float32 [32, 64], P(None, 'mp'), may hold values from -4 to 4
Outputs:
- grad_q_self: bfloat16 [4, 1024, 4096], P('dp', 'seq', 'mp')
- grad_k_self: bfloat16 [4, 1024, 4096], P('dp', 'seq', 'mp')
- grad_v_self: bfloat16 [4, 1024, 4096], P('dp', 'seq', 'mp')
- grad_q_cross: bfloat16 [4, 1024, 4096], P('dp', 'seq', 'mp')
- grad_k_cross: bfloat16 [4, 2048, 4096], P('dp', 'seq', 'mp')
- grad_v_cross: bfloat16 [4, 2048, 4096], P('dp', 'seq', 'mp')
- bias_grad: float32 [32, 64], P(None, 'mp')
Inputs may be any that keep to these rules, and one draw needn't show every extreme that they name: `dec_lengths`: row p lists the decoder lengths of the 16 examples of pack p in order; they sum to 1024 and the largest is exactly 640. `enc_lengths`: row p lists the encoder lengths of the same 16 examples in the same order; they sum to 2048. The example with 640 decoder rows has exactly 1280 encoder rows; every other example has at least as many encoder rows as decoder rows and at most three times as many.
All inputs are finite; a program needn't handle non-finite values.
Results may differ from a plain program's by a relative error of at most 0.039.
Values may be sent and summed in bfloat16 or wider, within the bound.
A program may use at most 128 MiB of HBM per device.

v0:
```python
import math
import jax
import jax.numpy as jnp
from jax import lax
from jax.sharding import PartitionSpec as P

HEAD_DIM = 64
BUCKETS = 32
DISTANCE = 128


def bucket_of(distances):
    exact_count = BUCKETS // 2
    bucketed = jnp.full(distances.shape, exact_count, jnp.int32)
    for level_index in range(1, BUCKETS - exact_count):
        threshold = math.ceil(
            exact_count * (DISTANCE / exact_count) ** (level_index / (BUCKETS - exact_count))
        )
        bucketed = bucketed + (distances >= threshold).astype(jnp.int32)
    return jnp.where(distances < exact_count, distances, bucketed)


def example_ids(total_rows, lengths):
    segment_ends = jnp.cumsum(lengths)
    positions = jnp.arange(total_rows, dtype=jnp.int32)
    return jnp.sum((positions[:, None] >= segment_ends[None, :]).astype(jnp.int32), axis=1)


def distance_table(rel_bias, offset_base, table_span):
    distances = offset_base + jnp.arange(table_span, dtype=jnp.int32)
    buckets = bucket_of(jnp.maximum(distances, 0))
    one_hot = (buckets[None, :] == jnp.arange(rel_bias.shape[0], dtype=jnp.int32)[:, None]).astype(
        jnp.float32
    )
    bias_table = jnp.einsum("bh,bl->hl", rel_bias, one_hot, precision=lax.Precision.HIGHEST)
    return (one_hot, bias_table)


def spread(bias_table, row_count, col_count):
    full_span = row_count + col_count - 1
    leading = bias_table.shape[:-1]
    tiled_rows = jnp.broadcast_to(bias_table[..., None, :], leading + (row_count, full_span))
    flat_rows = tiled_rows.reshape(leading + (row_count * full_span,))
    flat_rows = jnp.pad(flat_rows, [(0, 0)] * len(leading) + [(0, row_count)])
    skewed = flat_rows.reshape(leading + (row_count, full_span + 1))[..., :col_count]
    return skewed[..., ::-1]


def collapse(matrix, row_count, col_count):
    full_span = row_count + col_count - 1
    leading = matrix.shape[:-2]
    flipped = matrix[..., ::-1]
    padded = jnp.pad(flipped, [(0, 0)] * len(leading) + [(0, 0), (0, row_count)])
    flat_rows = padded.reshape(leading + (row_count * (full_span + 1),))[
        ..., : row_count * full_span
    ]
    return jnp.sum(flat_rows.reshape(leading + (row_count, full_span)), axis=-2)


def shard_group(shard_count, row_count):
    group_size = 1
    while group_size < shard_count and (
        shard_count % group_size != 0 or group_size * row_count < 384
    ):
        group_size += 1
    return group_size


def query_side(
    queries,
    out_grads,
    all_keys,
    all_values,
    key_ids,
    query_ids,
    query_start,
    rel_bias,
    block_rows,
    causal,
):
    row_count, head_count, head_size = queries.shape
    block_count = all_keys.shape[0] // block_rows
    query_pos = query_start + jnp.arange(row_count, dtype=jnp.int32)
    block_ids = jnp.arange(block_count, dtype=jnp.int32)

    def scores_of(block_id):
        key_first = block_id * block_rows
        key_block = lax.dynamic_slice_in_dim(all_keys, key_first, block_rows, 0)
        key_block_ids = lax.dynamic_slice_in_dim(key_ids, key_first, block_rows, 0)
        scores = jnp.einsum("thd,uhd->htu", queries, key_block, preferred_element_type=jnp.float32)
        allowed = query_ids[:, None] == key_block_ids[None, :]
        one_hot = jnp.zeros((1, 1), jnp.float32)
        if causal:
            key_pos = key_first + jnp.arange(block_rows, dtype=jnp.int32)
            allowed = allowed & (query_pos[:, None] >= key_pos[None, :])
            one_hot, bias_table = distance_table(
                rel_bias, query_start - key_first - (block_rows - 1), row_count + block_rows - 1
            )
            scores = scores + spread(bias_table, row_count, block_rows)
        return (jnp.where(allowed[None], scores, -1e30), one_hot)

    def stat_step(running, block_id):
        row_high, total_sum = running
        scores, unused_hot = scores_of(block_id)
        new_high = jnp.maximum(row_high, jnp.max(scores, axis=2))
        total_sum = total_sum * jnp.exp(row_high - new_high) + jnp.sum(
            jnp.exp(scores - new_high[:, :, None]), axis=2
        )
        return ((new_high, total_sum), None)

    start_state = (
        jnp.full((head_count, row_count), -1e30, jnp.float32),
        jnp.zeros((head_count, row_count), jnp.float32),
    )
    (row_high, total_sum), unused_stats = lax.scan(stat_step, start_state, block_ids)

    def weights_of(scores):
        return jnp.exp(scores - row_high[:, :, None]) / total_sum[:, :, None]

    def out_step(summed, block_id):
        scores, unused_hot = scores_of(block_id)
        narrow_weights = weights_of(scores).astype(jnp.bfloat16)
        value_block = lax.dynamic_slice_in_dim(all_values, block_id * block_rows, block_rows, 0)
        return (
            summed
            + jnp.einsum(
                "htu,uhd->thd", narrow_weights, value_block, preferred_element_type=jnp.float32
            ),
            None,
        )

    summed, unused_outs = lax.scan(
        out_step, jnp.zeros((row_count, head_count, head_size), jnp.float32), block_ids
    )
    outputs = summed.astype(jnp.bfloat16)
    row_delta = jnp.einsum("thd,thd->ht", out_grads, outputs, preferred_element_type=jnp.float32)

    def grad_step(running, block_id):
        query_grad, bias_grad_sum = running
        scores, one_hot = scores_of(block_id)
        weights = weights_of(scores)
        narrow_weights = weights.astype(jnp.bfloat16)
        key_block = lax.dynamic_slice_in_dim(all_keys, block_id * block_rows, block_rows, 0)
        value_block = lax.dynamic_slice_in_dim(all_values, block_id * block_rows, block_rows, 0)
        weight_grads = jnp.einsum(
            "thd,uhd->htu", out_grads, value_block, preferred_element_type=jnp.float32
        )
        score_grads = weights * (weight_grads - row_delta[:, :, None])
        narrow_grads = score_grads.astype(jnp.bfloat16)
        query_grad = query_grad + jnp.einsum(
            "htu,uhd->thd", narrow_grads, key_block, preferred_element_type=jnp.float32
        )
        if causal:
            bias_grad_sum = bias_grad_sum + jnp.einsum(
                "hl,bl->bh",
                collapse(score_grads, row_count, block_rows),
                one_hot,
                precision=lax.Precision.HIGHEST,
            )
        key_term = jnp.einsum(
            "htu,thd->uhd", narrow_grads, queries, preferred_element_type=jnp.float32
        )
        value_term = jnp.einsum(
            "htu,thd->uhd", narrow_weights, out_grads, preferred_element_type=jnp.float32
        )
        grad_term = jnp.concatenate(
            [
                key_term.reshape(block_rows, head_count * head_size),
                value_term.reshape(block_rows, head_count * head_size),
            ],
            axis=1,
        ).astype(jnp.bfloat16)
        return ((query_grad, bias_grad_sum), grad_term)

    grad_state = (
        jnp.zeros((row_count, head_count, head_size), jnp.float32),
        jnp.zeros((rel_bias.shape[0], head_count), jnp.float32),
    )
    (query_grad, bias_grad_sum), grad_terms = lax.scan(grad_step, grad_state, block_ids)
    grad_terms = grad_terms.reshape(block_count * block_rows, 2 * head_count * head_size)
    query_grad = query_grad.astype(jnp.bfloat16).reshape(row_count, head_count * head_size)
    return (query_grad, grad_terms, bias_grad_sum, (row_high, total_sum, row_delta))


def on_device(
    q_self,
    k_self,
    v_self,
    out_grad_self,
    q_cross,
    k_cross,
    v_cross,
    out_grad_cross,
    dec_lengths,
    enc_lengths,
    rel_bias,
):
    seq_count = lax.axis_size("seq")
    seq_place = lax.axis_index("seq")
    dec_rows = q_self.shape[1]
    enc_rows = k_cross.shape[1]
    feature_count = q_self.shape[2]
    head_count = feature_count // HEAD_DIM
    dec_total = dec_rows * seq_count
    enc_total = enc_rows * seq_count
    dec_start = seq_place * dec_rows
    dec_ids = example_ids(dec_total, dec_lengths[0])
    enc_ids = example_ids(enc_total, enc_lengths[0])
    my_dec_ids = lax.dynamic_slice_in_dim(dec_ids, dec_start, dec_rows, 0)

    def split_heads(tensor):
        return tensor.reshape(tensor.shape[0] * tensor.shape[1], head_count, HEAD_DIM)

    gathered = (
        lax.all_gather(k_self, "seq", axis=1, tiled=True),
        lax.all_gather(v_self, "seq", axis=1, tiled=True),
        lax.all_gather(k_cross, "seq", axis=1, tiled=True),
        lax.all_gather(v_cross, "seq", axis=1, tiled=True),
    )
    self_group = shard_group(seq_count, dec_rows)
    cross_group = shard_group(seq_count, enc_rows)
    self_dq, self_terms, self_bias, self_stats = query_side(
        split_heads(q_self),
        split_heads(out_grad_self),
        split_heads(gathered[0]),
        split_heads(gathered[1]),
        dec_ids,
        my_dec_ids,
        dec_start,
        rel_bias,
        self_group * dec_rows,
        True,
    )
    cross_dq, cross_terms, unused_bias, cross_stats = query_side(
        split_heads(q_cross),
        split_heads(out_grad_cross),
        split_heads(gathered[2]),
        split_heads(gathered[3]),
        enc_ids,
        my_dec_ids,
        dec_start,
        rel_bias,
        cross_group * enc_rows,
        False,
    )
    self_sums = lax.psum_scatter(
        self_terms.astype(jnp.float32).astype(jnp.bfloat16), "seq", scatter_dimension=0, tiled=True
    ).astype(jnp.float32)
    cross_sums = lax.psum_scatter(
        cross_terms.astype(jnp.float32).astype(jnp.bfloat16), "seq", scatter_dimension=0, tiled=True
    ).astype(jnp.float32)
    self_key_grad = self_sums[:, :feature_count]
    self_value_grad = self_sums[:, feature_count:]
    cross_key_grad = cross_sums[:, :feature_count]
    cross_value_grad = cross_sums[:, feature_count:]
    bias_total = lax.psum(self_bias, ("dp", "seq"))
    bias_grad = bias_total * (1.0 / math.sqrt(lax.axis_size("dp") * dec_total))
    return (
        self_dq.reshape(1, dec_rows, feature_count),
        self_key_grad.reshape(1, dec_rows, feature_count).astype(jnp.bfloat16),
        self_value_grad.reshape(1, dec_rows, feature_count).astype(jnp.bfloat16),
        cross_dq.reshape(1, dec_rows, feature_count),
        cross_key_grad.reshape(1, enc_rows, feature_count).astype(jnp.bfloat16),
        cross_value_grad.reshape(1, enc_rows, feature_count).astype(jnp.bfloat16),
        bias_grad,
    )


def solution(mesh):
    return jax.shard_map(
        on_device,
        mesh=mesh,
        in_specs=(
            P("dp", "seq", "mp"),
            P("dp", "seq", "mp"),
            P("dp", "seq", "mp"),
            P("dp", "seq", "mp"),
            P("dp", "seq", "mp"),
            P("dp", "seq", "mp"),
            P("dp", "seq", "mp"),
            P("dp", "seq", "mp"),
            P("dp", None),
            P("dp", None),
            P(None, "mp"),
        ),
        out_specs=(
            P("dp", "seq", "mp"),
            P("dp", "seq", "mp"),
            P("dp", "seq", "mp"),
            P("dp", "seq", "mp"),
            P("dp", "seq", "mp"),
            P("dp", "seq", "mp"),
            P(None, "mp"),
        ),
        check_vma=False,
    )
```

profile of v0, /device:TPU:2, one launch (start us, length us, event | category | flops | bytes accessed | tf_op | source)
XLA Modules:
  0.0 455.4 jit_solution(5825784003897655049)
XLA Ops:
  17.9 34.6 %all-gather.5.cloned.1.call-done = bf16[1,1024,1024]{2,1,0:T(8,128)(2,1)} async-done(((bf16[1,64,1024]{2,1,0:T(8,128)(2,1)}), bf16[1,1024,1024]{2,1,0:T(8,128)(2,1)}) %all-gather.5.cloned.1.call-update) | async-done | bytes 2097168 | tf_op jit(solution)/shard_map/all_gather | solution.py:215
  52.6 3.9 copy.70
  56.5 31.9 %while.91 = (s32[]{:T(128)}, f32[16,64]{1,0:T(8,128)S(1)}, f32[16,64]{1,0:T(8,128)S(1)}, s32[64]{0:T(128)S(1)}, s32[2]{0:T(128)S(1)}, /*index=5*/s32[1024]{0:T(1...) while((s32[]{:T(128)}, f32[16,64]{1,0:T(8,128)S(1)}, ...), condition=%wide.region_5.6_spmd.clone.clone.clone, body=%wide.region_2.0_spmd.clone.clone.clone.sunk | while | flops 73413688 | bytes 34665884 | solution.py:115
  58.3 2.5 reshape.719
  62.6 2.4 reshape.720
  66.6 2.5 rev.40
  69.2 2.4 fusion.207
  74.3 2.5 reshape.719
  78.6 2.4 reshape.720
  82.6 2.5 rev.40
  85.1 2.4 fusion.207
  88.4 4.1 all-gather.7.cloned.1.call-done
  92.5 3.9 copy.74
  96.4 34.2 %while.92 = (s32[]{:T(128)}, f32[64,16,64]{0,2,1:T(8,128)}, s32[2]{0:T(128)S(1)}, bf16[1024,16,64]{0,2,1:T(8,128)(2,1)}, s32[64]{0:T(128)S(1)}, /*index=5*/s32[1...) while((s32[]{:T(128)}, f32[64,16,64]{0,2,1:T(8,128)}, ...), condition=%wide.region_7.8_spmd.clone.clone.clone, body=%wide.region_6.7_spmd.clone.clone.clone.sunk | while | flops 140648496 | bytes 34098144 | solution.py:132
  98.3 2.5 reshape.721
  102.6 2.5 reshape.722
  106.7 2.5 rev.41
  109.2 3.4 fusion.213
  115.4 2.5 reshape.721
  117.9 1.9 pad.57
  119.7 2.5 reshape.722
  123.8 2.5 rev.41
  126.3 3.4 fusion.213
  131.7 80.7 %while.93 = (s32[]{:T(128)}, f32[64,16,64]{0,2,1:T(8,128)}, f32[32,16]{0,1:T(8,128)S(1)}, bf16[2,512,2048]{2,1,0:T(8,128)(2,1)}, s32[2]{0:T(128)S(1)}, /*index=5...) while((s32[]{:T(128)}, f32[64,16,64]{0,2,1:T(8,128)}, ...), condition=%wide.region_10.11_spmd.clone.clone.clone, body=%wide.region_8.10_spmd.clone.clone.clone.sunk | while | flops 353446976 | bytes 101543680 | solution.py:179
  133.7 2.5 reshape.723
  138.1 2.5 reshape.724
  142.1 2.5 rev.42
  144.6 2.7 fusion.226
  151.9 2.3 convolution_convert_fusion.11
  154.3 2.5 rev.43
  158.2 2.4 copy.117
  160.6 1.9 pad.61
  162.5 2.3 reshape.725
  164.8 3.7 reshape.726
  168.9 3.3 constant_dynamic-update-slice_fusion.5
  174.1 2.5 reshape.723
  178.4 2.5 reshape.724
  182.4 2.5 rev.42
  184.9 2.7 fusion.226
  192.3 2.3 convolution_convert_fusion.11
  194.6 2.5 rev.43
  198.5 2.4 copy.117
  200.9 1.9 pad.61
  202.8 2.3 reshape.725
  205.1 3.7 reshape.726
  209.2 3.3 constant_dynamic-update-slice_fusion.5
  212.6 6.7 %copy.79 = bf16[1,2048,1024]{1,2,0:T(8,128)(2,1)} copy(bf16[1,2048,1024]{2,1,0:T(8,128)(2,1)} %all-gather.9.cloned.1.call-done) | data formatting | bytes 8388608 | tf_op jit(solution)/shard_map/all_gather | solution.py:217
  219.4 15.2 %while.88 = (s32[]{:T(128)}, f32[16,64]{1,0:T(8,128)S(1)}, f32[16,64]{1,0:T(8,128)S(1)}, s32[64]{0:T(128)S(1)}, s32[4]{0:T(128)S(1)}, /*index=5*/s32[2048]{0:T(1...) while((s32[]{:T(128)}, f32[16,64]{1,0:T(8,128)S(1)}, ...), condition=%wide.region_17.18_spmd.clone, body=%wide.region_14.17_spmd.clone.sunk | while | flops 69768200 | bytes 5532106 | solution.py:115
  234.6 6.6 %copy.83 = bf16[1,2048,1024]{1,2,0:T(8,128)(2,1)} copy(bf16[1,2048,1024]{2,1,0:T(8,128)(2,1)} %all-gather.11.cloned.1.call-done) | data formatting | bytes 8388608 | tf_op jit(solution)/shard_map/all_gather | solution.py:218
  241.3 16.1 %while.89 = (s32[]{:T(128)}, f32[64,16,64]{0,2,1:T(8,128)S(1)}, s32[4]{0:T(128)S(1)}, bf16[2048,16,64]{0,2,1:T(8,128)(2,1)}, s32[64]{0:T(128)S(1)}, /*index=5*/s...) while((s32[]{:T(128)}, f32[64,16,64]{0,2,1:T(8,128)S(1)}, ...), condition=%wide.region_19.20_spmd.clone, body=%wide.region_18.19_spmd.clone.sunk | while | flops 136478720 | bytes 2834388 | solution.py:132
  242.7 2.6 fusion.191
  246.7 2.6 fusion.191
  250.8 2.5 fusion.191
  254.8 2.6 fusion.191
  257.5 54.1 %while.90 = (s32[]{:T(128)}, f32[64,16,64]{0,2,1:T(8,128)S(1)}, bf16[4,512,2048]{2,1,0:T(8,128)(2,1)}, s32[4]{0:T(128)S(1)}, bf16[2048,16,64]{0,2,1:T(8,128)(2,1...) while((s32[]{:T(128)}, f32[64,16,64]{0,2,1:T(8,128)S(1)}, ...), condition=%wide.region_21.22_spmd.clone, body=%wide.region_20.21_spmd.clone.sunk | while | flops 344621056 | bytes 28396028 | solution.py:179
  258.9 1.9 fusion.202
  266.6 2.9 copy.116
  272.5 1.9 fusion.202
  280.2 2.9 copy.116
  286.0 1.9 fusion.202
  293.6 2.9 copy.116
  299.5 1.9 fusion.202
  307.1 2.9 copy.116
  313.4 130.1 %psum.7 = f32[32,16]{0,1:T(8,128)S(1)} all-reduce(f32[32,16]{0,1:T(8,128)S(1)} %get-tuple-element.693), channel_id=1, replica_groups=mesh['dp'=4,'seq'=16,'mp'=4] {'dp','seq'}, use_global_device_ids=true, to_apply=%region_23.24 | all-reduce | flops 512 | bytes 4096 | tf_op jit(solution)/shard_map/psum | solution.py:256
  (278 shorter events, 107.5 us)
Async XLA Ops:
  7.2 9.6 %copy-start.19 = (bf16[1,64,1024]{2,1,0:T(8,128)(2,1)S(1)}, bf16[1,64,1024]{2,1,0:T(8,128)(2,1)}, u32[]{:S(2)}) copy-start(bf16[1,64,1024]{2,1,0:T(8,128)(2,1)} %param.27) | copy-start | bytes 393220
  7.2 45.4 %all-gather.5.cloned.1.call-start = ((), (), s32[]{:S(2)}) async-start(), calls=%async_computation.2 | async-start | bytes 2228224 | tf_op jit(solution)/shard_map/all_gather | solution.py:215
  7.9 84.5 %all-gather.7.cloned.1.call-start = ((), (), s32[]{:S(2)}) async-start(), calls=%async_computation.3 | async-start | bytes 2228224 | tf_op jit(solution)/shard_map/all_gather | solution.py:216
  8.7 203.9 %all-gather.9.cloned.1.call-start = ((), (), s32[]{:S(2)}) async-start(), calls=%async_computation.5 | async-start | bytes 4456448 | tf_op jit(solution)/shard_map/all_gather | solution.py:217
  9.4 225.2 %all-gather.11.cloned.1.call-start = ((), (), s32[]{:S(2)}) async-start(), calls=%async_computation.6 | async-start | bytes 4456448 | tf_op jit(solution)/shard_map/all_gather | solution.py:218
  10.0 435.0 %reduce-scatter.3.cloned.1.call-start = ((), (), s32[]{:S(2)}) async-start(), calls=%async_computation.4 | async-start | bytes 4456448 | tf_op jit(solution)/shard_map/reduce_scatter | solution.py:246
  17.0 39.5 %copy-start.7 = (bf16[1,64,1024]{1,2,0:T(8,128)(2,1)}, bf16[1,64,1024]{1,2,0:T(8,128)(2,1)S(1)}, u32[]{:S(2)}) copy-start(bf16[1,64,1024]{1,2,0:T(8,128)(2,1)S(1)} %copy.81) | copy-start | bytes 393220
  17.9 38.6 %copy-start.12 = (f32[32,16]{0,1:T(8,128)S(1)}, f32[32,16]{0,1:T(8,128)}, u32[]{:S(2)}) copy-start(f32[32,16]{0,1:T(8,128)} %param.33) | copy-start | bytes 6148
  65.0 1.6 slice-start
  81.0 1.6 slice-start
  105.1 1.6 slice-start.1
  106.7 2.5 copy-start.15
  112.6 0.8 copy-start.16
  122.2 1.6 slice-start.1
  123.8 2.5 copy-start.15
  129.7 0.8 copy-start.16
  131.9 12.7 %copy-start.9 = (bf16[64,16,64]{0,2,1:T(8,128)(2,1)}, bf16[64,16,64]{0,2,1:T(8,128)(2,1)S(1)}, u32[]{:S(2)}) copy-start(bf16[64,16,64]{0,2,1:T(8,128)(2,1)S(1)} %get-tuple-element.1967) | copy-start | bytes 393220 | tf_op jit(solution)/shard_map/while
  140.5 1.6 slice-start.2
  147.3 1.6 copy-start.2
  148.8 1.6 copy-start
  148.9 1.7 copy-start.3
  151.1 0.8 copy-start.4
  168.9 3.3 copy-start.10
  172.3 12.7 %copy-start.9 = (bf16[64,16,64]{0,2,1:T(8,128)(2,1)}, bf16[64,16,64]{0,2,1:T(8,128)(2,1)S(1)}, u32[]{:S(2)}) copy-start(bf16[64,16,64]{0,2,1:T(8,128)(2,1)S(1)} %get-tuple-element.1967) | copy-start | bytes 393220 | tf_op jit(solution)/shard_map/while
  180.8 1.6 slice-start.2
  187.6 1.6 copy-start.2
  189.2 1.6 copy-start
  189.2 1.7 copy-start.3
  191.4 0.8 copy-start.4
  209.2 3.3 copy-start.10
  212.5 6.9 %copy-start.11 = (bf16[64,16,64]{2,0,1:T(8,128)(2,1)S(1)}, bf16[64,16,64]{2,0,1:T(8,128)(2,1)}, u32[]{:S(2)}) copy-start(bf16[64,16,64]{2,0,1:T(8,128)(2,1)} %copy.82) | copy-start | bytes 393220
  212.5 6.8 %copy-start.13 = (f32[16,64]{1,0:T(8,128)S(1)}, f32[16,64]{1,0:T(8,128)}, u32[]{:S(2)}) copy-start(f32[16,64]{1,0:T(8,128)} %custom-call.5) | copy-start | bytes 12292
  212.5 6.8 %copy-start.17 = (f32[16,64]{1,0:T(8,128)S(1)}, f32[16,64]{1,0:T(8,128)}, u32[]{:S(2)}) copy-start(f32[16,64]{1,0:T(8,128)} %custom-call.6) | copy-start | bytes 12292
  212.5 6.8 %copy-start.18 = (s32[2048]{0:T(1024)S(1)}, s32[2048]{0:T(1024)}, u32[]{:S(2)}) copy-start(s32[2048]{0:T(1024)} %convert_reduce_fusion) | copy-start | bytes 24580
  212.5 234.2 %reduce-scatter.5.cloned.1.call-start = ((), (), s32[]{:S(2)}) async-start(), calls=%async_computation.7 | async-start | bytes 8912896 | tf_op jit(solution)/shard_map/reduce_scatter | solution.py:249
  234.6 6.7 %copy-start.14 = (f32[64,16,64]{0,2,1:T(8,128)S(1)}, f32[64,16,64]{0,2,1:T(8,128)}, u32[]{:S(2)}) copy-start(f32[64,16,64]{0,2,1:T(8,128)} %custom-call.7) | copy-start | bytes 786436
  241.3 16.1 %copy-start.1 = (bf16[1,64,1024]{1,2,0:T(8,128)(2,1)S(1)}, bf16[1,64,1024]{1,2,0:T(8,128)(2,1)}, u32[]{:S(2)}) copy-start(bf16[1,64,1024]{1,2,0:T(8,128)(2,1)} %copy.84) | copy-start | bytes 393220
  241.3 16.2 %copy-start.6 = (f32[64,16,64]{0,2,1:T(8,128)S(1)}, f32[64,16,64]{0,2,1:T(8,128)}, u32[]{:S(2)}) copy-start(f32[64,16,64]{0,2,1:T(8,128)} %custom-call.8) | copy-start | bytes 786436
  241.3 16.2 %copy-start.8 = (bf16[1,64,1024]{1,2,0:T(8,128)(2,1)S(1)}, bf16[1,64,1024]{1,2,0:T(8,128)(2,1)}, u32[]{:S(2)}) copy-start(bf16[1,64,1024]{1,2,0:T(8,128)(2,1)} %copy-done.7) | copy-start | bytes 393220
  311.6 1.0 copy-start.5
Sparse Core Ops, SparseCore 0:
  9.8 42.6 all-gather.4
  54.4 38.0 all-gather.6
  94.3 40.5 all-gather.8
  136.5 40.8 all-gather.10
  212.6 61.6 reduce-scatter.2
  311.7 69.7 reduce-scatter.4
where the time goes:
time: 458 us; the launch traced here: 455 us
  local copies, waits for them, and re-layouts  170 us (37%)
  blocking collectives  130 us (28%)
  matrix products  67.9 us (15%)
  waiting for transfers between devices  41.4 us (9%)
  other arithmetic  17.8 us (4%)
  between operations  14.5 us (3%)
  loops' own time  13.3 us (3%)
    psum x1, blocking collectives, on_device(): bias_total = lax.psum(self_bias, ('dp', 'seq'))  130 us
    all_gather x1, waiting for transfers between devices, on_device(): lax.all_gather(k_self, 'seq', axis=1, tiled=True)  34.6 us
    dynamic_update_slice x12, local copies, waits for them, and re-layouts, query_side(): lax.scan(grad_step, grad_state, block_ids)  29.1 us
    dot_general x12, matrix products, scores_of(): jnp.einsum('thd,uhd->htu', queries, key_block, preferred_element_type=jnp...  24.8 us
    dot_general x6, matrix products, out_step(): jnp.einsum('htu,uhd->thd', narrow_weights, value_block, preferred_element...  17.1 us
    rev x6, local copies, waits for them, and re-layouts, spread(): return skewed[..., ::-1]  15.1 us
    reshape x6, local copies, waits for them, and re-layouts, spread(): flat_rows = tiled_rows.reshape(leading + (row_count * full_span,))  14.9 us
    reshape x6, local copies, waits for them, and re-layouts, spread(): flat_rows.reshape(leading + (row_count, full_span + 1))[..., :col_count]  14.6 us
  transfers between devices with their start and end apart: 6, of which 2 were waited for; matrix products, arithmetic and copies ran while one was open for 52% of the time, Pallas kernels for 0%

commit v1 on v0

--- a/solution.py
+++ b/solution.py
@@ -212,7 +212,9 @@
         return tensor.reshape(tensor.shape[0] * tensor.shape[1], head_count, HEAD_DIM)
 
     gathered = (
-        lax.all_gather(k_self, "seq", axis=1, tiled=True),
+        jnp.concatenate(
+            lax.all_to_all(jnp.stack([k_self] * lax.axis_size("seq")), "seq", 0, 0), axis=1
+        ),
         lax.all_gather(v_self, "seq", axis=1, tiled=True),
         lax.all_gather(k_cross, "seq", axis=1, tiled=True),
         lax.all_gather(v_cross, "seq", axis=1, tiled=True),

time: 458 us -> 485 us (1.059)
  waiting for transfers between devices: 41.4 us -> 56.5 us
  starting transfers between devices: 0.23 us -> 8.91 us
    all_to_all x0 -> x1, waiting for transfers between devices: none -> 54.3 us  [on_device(): lax.all_to_all(jnp.stack([k_self] * lax.axis_size('seq')), 'seq', 0, 0)]
    all_gather x1 -> x0, waiting for transfers between devices: 34.6 us -> none  [on_device(): lax.all_gather(k_self, 'seq', axis=1, tiled=True)]
    all_to_all x0 -> x1, starting transfers between devices: none -> 8.71 us  [on_device(): lax.all_to_all(jnp.stack([k_self] * lax.axis_size('seq')), 'seq', 0, 0)]
    another operation x2 -> x4, local copies, waits for them, and re-layouts: 1.47 us -> 6.68 us  [the longest x1 4 us: split_heads(): tensor.reshape(tensor.shape[0] * tensor.shape[1], head_count, HEAD_DIM)]
  transfers between devices with their start and end apart: 6 -> 6, of which waited for: 2 -> 1; matrix products, arithmetic and copies ran while one was open for 52% -> 50% of each run, Pallas kernels for 0% -> 0%
where the time goes in v1:
time: 485 us; the launch traced here: 482 us
  local copies, waits for them, and re-layouts  174 us (36%)
  blocking collectives  130 us (27%)
  matrix products  67.9 us (14%)
  waiting for transfers between devices  56.5 us (12%)
  other arithmetic  17.7 us (4%)
  between operations  14.2 us (3%)
  loops' own time  13.1 us (3%)
  starting transfers between devices  8.91 us (2%)
    psum x1, blocking collectives, on_device(): bias_total = lax.psum(self_bias, ('dp', 'seq'))  130 us
    all_to_all x1, waiting for transfers between devices, on_device(): lax.all_to_all(jnp.stack([k_self] * lax.axis_size('seq')), 'seq', 0, 0)  54.3 us
    dynamic_update_slice x12, local copies, waits for them, and re-layouts, query_side(): lax.scan(grad_step, grad_state, block_ids)  29 us
    dot_general x12, matrix products, scores_of(): jnp.einsum('thd,uhd->htu', queries, key_block, preferred_element_type=jnp...  24.8 us
    dot_general x6, matrix products, out_step(): jnp.einsum('htu,uhd->thd', narrow_weights, value_block, preferred_element...  17 us
    rev x6, local copies, waits for them, and re-layouts, spread(): return skewed[..., ::-1]  15.2 us
    reshape x6, local copies, waits for them, and re-layouts, spread(): flat_rows = tiled_rows.reshape(leading + (row_count * full_span,))  14.9 us
    reshape x6, local copies, waits for them, and re-layouts, spread(): flat_rows.reshape(leading + (row_count, full_span + 1))[..., :col_count]  14.7 us
  transfers between devices with their start and end apart: 6, of which 1 were waited for; matrix products, arithmetic and copies ran while one was open for 50% of the time, Pallas kernels for 0%

profile of v1, /device:TPU:2, one launch (start us, length us, event | category | flops | bytes accessed | tf_op | source)
XLA Modules:
  0.0 482.3 jit_solution(10161582704797826546)
XLA Ops:
  8.6 2.5 stack.2
  11.2 8.7 %all-to-all-start = ((bf16[16,1,64,1024]{3,2,1,0:T(8,128)(2,1)}), bf16[16,1,64,1024]{3,2,1,0:T(8,128)(2,1)S(1)}, u32[]{:S(2)}, u32[]{:S(2)}) async-start(bf16[16,1,64,1024]{3,2,1,0:T(8,128)(2,1)} %stack.2), calls=%async_computation | async-start | bytes 4194304 | tf_op jit(solution)/shard_map/all_to_all | solution.py:216
  24.6 54.3 %all-to-all-done = bf16[16,1,64,1024]{3,2,1,0:T(8,128)(2,1)S(1)} async-done(((bf16[16,1,64,1024]{3,2,1,0:T(8,128)(2,1)}), bf16[16,1,64,1024]{3,2,1,0:T(8,128)(2,1)S(1)}, u32[]{:S(2)}, u32[]{:S(2)}) %all-to-all-start) | async-done | bytes 2097184 | tf_op jit(solution)/shard_map/all_to_all | solution.py:216
  78.9 4.0 reshape_reshape.9
  82.9 5.5 %copy.102 = bf16[1024,16,64]{0,2,1:T(8,128)(2,1)} copy(bf16[1024,16,64]{2,1,0:T(8,128)(2,1)} %reshape_reshape.9) | data formatting | bytes 4194304
  88.4 32.0 %while.91 = (s32[]{:T(128)}, f32[16,64]{1,0:T(8,128)S(1)}, f32[16,64]{1,0:T(8,128)S(1)}, s32[64]{0:T(128)S(1)}, s32[2]{0:T(128)S(1)}, /*index=5*/s32[1024]{0:T(1...) while((s32[]{:T(128)}, f32[16,64]{1,0:T(8,128)S(1)}, ...), condition=%wide.region_5.6_spmd.clone.clone.clone, body=%wide.region_2.0_spmd.clone.clone.clone.sunk | while | flops 73413688 | bytes 34665884 | solution.py:115
  90.2 2.4 reshape.718
  94.5 2.4 reshape.719
  98.5 2.6 rev.40
  101.1 2.5 fusion.207
  106.2 2.4 reshape.718
  108.6 1.9 pad.56
  110.5 2.4 reshape.719
  114.5 2.6 rev.40
  117.1 2.5 fusion.207
  120.4 4.0 copy.98
  124.4 33.9 %while.92 = (s32[]{:T(128)}, f32[64,16,64]{0,2,1:T(8,128)}, s32[2]{0:T(128)S(1)}, bf16[1024,16,64]{0,2,1:T(8,128)(2,1)}, s32[64]{0:T(128)S(1)}, /*index=5*/s32[1...) while((s32[]{:T(128)}, f32[64,16,64]{0,2,1:T(8,128)}, ...), condition=%wide.region_7.8_spmd.clone.clone.clone, body=%wide.region_6.7_spmd.clone.clone.clone.sunk | while | flops 140648496 | bytes 34098144 | solution.py:132
  126.2 2.5 reshape.720
  130.5 2.5 reshape.721
  134.6 2.5 rev.41
  137.1 3.3 fusion.213
  143.1 2.5 reshape.720
  147.5 2.5 reshape.721
  151.6 2.5 rev.41
  154.1 3.4 fusion.213
  159.5 80.8 %while.93 = (s32[]{:T(128)}, f32[64,16,64]{0,2,1:T(8,128)}, f32[32,16]{0,1:T(8,128)S(1)}, bf16[2,512,2048]{2,1,0:T(8,128)(2,1)}, s32[2]{0:T(128)S(1)}, /*index=5...) while((s32[]{:T(128)}, f32[64,16,64]{0,2,1:T(8,128)}, ...), condition=%wide.region_10.11_spmd.clone.clone.clone, body=%wide.region_8.10_spmd.clone.clone.clone.sunk | while | flops 353446976 | bytes 101543680 | solution.py:179
  161.5 2.5 reshape.722
  165.9 2.5 reshape.723
  169.9 2.5 rev.42
  172.4 2.7 fusion.226
  179.8 2.3 convolution_convert_fusion.11
  182.1 2.5 rev.43
  186.0 2.4 copy.143
  190.3 2.3 reshape.724
  192.6 3.7 reshape.725
  196.7 3.2 constant_dynamic-update-slice_fusion.5
  201.8 2.5 reshape.722
  206.1 2.5 reshape.723
  210.2 2.5 rev.42
  212.7 2.7 fusion.226
  220.0 2.3 convolution_convert_fusion.11
  222.4 2.5 rev.43
  226.3 2.4 copy.143
  230.6 2.3 reshape.724
  232.9 3.7 reshape.725
  237.0 3.3 constant_dynamic-update-slice_fusion.5
  240.4 6.7 %copy.105 = bf16[1,2048,1024]{1,2,0:T(8,128)(2,1)} copy(bf16[1,2048,1024]{2,1,0:T(8,128)(2,1)} %all-gather.6.cloned.1.call-done) | data formatting | bytes 8388608 | tf_op jit(solution)/shard_map/all_gather | solution.py:219
  247.2 15.2 %while.88 = (s32[]{:T(128)}, f32[16,64]{1,0:T(8,128)S(1)}, f32[16,64]{1,0:T(8,128)S(1)}, s32[64]{0:T(128)S(1)}, s32[4]{0:T(128)S(1)}, /*index=5*/s32[2048]{0:T(1...) while((s32[]{:T(128)}, f32[16,64]{1,0:T(8,128)S(1)}, ...), condition=%wide.region_17.18_spmd.clone, body=%wide.region_14.17_spmd.clone.sunk | while | flops 69768200 | bytes 5532106 | solution.py:115
  262.5 6.6 %copy.109 = bf16[1,2048,1024]{1,2,0:T(8,128)(2,1)} copy(bf16[1,2048,1024]{2,1,0:T(8,128)(2,1)} %all-gather.8.cloned.1.call-done) | data formatting | bytes 8388608 | tf_op jit(solution)/shard_map/all_gather | solution.py:220
  269.1 16.1 %while.89 = (s32[]{:T(128)}, f32[64,16,64]{0,2,1:T(8,128)S(1)}, s32[4]{0:T(128)S(1)}, bf16[2048,16,64]{0,2,1:T(8,128)(2,1)}, s32[64]{0:T(128)S(1)}, /*index=5*/s...) while((s32[]{:T(128)}, f32[64,16,64]{0,2,1:T(8,128)S(1)}, ...), condition=%wide.region_19.20_spmd.clone, body=%wide.region_18.19_spmd.clone.sunk | while | flops 136478720 | bytes 2834388 | solution.py:132
  270.5 2.6 fusion.191
  274.6 2.6 fusion.191
  278.6 2.6 fusion.191
  282.6 2.6 fusion.191
  285.3 54.1 %while.90 = (s32[]{:T(128)}, f32[64,16,64]{0,2,1:T(8,128)S(1)}, bf16[4,512,2048]{2,1,0:T(8,128)(2,1)}, s32[4]{0:T(128)S(1)}, bf16[2048,16,64]{0,2,1:T(8,128)(2,1...) while((s32[]{:T(128)}, f32[64,16,64]{0,2,1:T(8,128)S(1)}, ...), condition=%wide.region_21.22_spmd.clone, body=%wide.region_20.21_spmd.clone.sunk | while | flops 344621056 | bytes 28396028 | solution.py:179
  286.8 1.9 fusion.202
  294.5 3.0 copy.142
  300.3 1.9 fusion.202
  308.0 2.9 copy.142
  313.8 1.9 fusion.202
  321.5 2.9 copy.142
  327.3 1.9 fusion.202
  335.0 2.9 copy.142
  341.3 129.5 %psum.7 = f32[32,16]{0,1:T(8,128)S(1)} all-reduce(f32[32,16]{0,1:T(8,128)S(1)} %get-tuple-element.693), channel_id=1, replica_groups=mesh['dp'=4,'seq'=16,'mp'=4] {'dp','seq'}, use_global_device_ids=true, to_apply=%region_23.24 | all-reduce | flops 512 | bytes 4096 | tf_op jit(solution)/shard_map/psum | solution.py:258
  (289 shorter events, 106.6 us)
Async XLA Ops:
  7.2 113.3 %all-gather.4.cloned.1.call-start = ((), (), s32[]{:S(2)}) async-start(), calls=%async_computation.3 | async-start | bytes 2228224 | tf_op jit(solution)/shard_map/all_gather | solution.py:218
  7.9 232.5 %all-gather.6.cloned.1.call-start = ((), (), s32[]{:S(2)}) async-start(), calls=%async_computation.5 | async-start | bytes 4456448 | tf_op jit(solution)/shard_map/all_gather | solution.py:219
  11.2 9.7 %copy-start.23 = (s32[1,16]{1,0:T(1,128)S(1)}, s32[1,16]{1,0:T(1,128)}, u32[]{:S(2)}) copy-start(s32[1,16]{1,0:T(1,128)} %param.31) | copy-start | bytes 196
  11.2 9.9 %copy-start.24 = (s32[1,16]{1,0:T(1,128)S(1)}, s32[1,16]{1,0:T(1,128)}, u32[]{:S(2)}) copy-start(s32[1,16]{1,0:T(1,128)} %param.32) | copy-start | bytes 196
  11.2 10.1 %copy-start.19 = (bf16[1,64,1024]{2,1,0:T(8,128)(2,1)S(1)}, bf16[1,64,1024]{2,1,0:T(8,128)(2,1)}, u32[]{:S(2)}) copy-start(bf16[1,64,1024]{2,1,0:T(8,128)(2,1)} %param.26) | copy-start | bytes 393220
  11.2 10.3 %copy-start.20 = (bf16[1,64,1024]{2,1,0:T(8,128)(2,1)S(1)}, bf16[1,64,1024]{2,1,0:T(8,128)(2,1)}, u32[]{:S(2)}) copy-start(bf16[1,64,1024]{2,1,0:T(8,128)(2,1)} %param.30) | copy-start | bytes 393220
  11.2 11.2 %copy-start.21 = (bf16[1,64,1024]{2,1,0:T(8,128)(2,1)S(1)}, bf16[1,64,1024]{2,1,0:T(8,128)(2,1)}, u32[]{:S(2)}) copy-start(bf16[1,64,1024]{2,1,0:T(8,128)(2,1)} %param.23) | copy-start | bytes 393220
  11.2 11.5 %copy-start.22 = (bf16[1,64,1024]{2,1,0:T(8,128)(2,1)S(1)}, bf16[1,64,1024]{2,1,0:T(8,128)(2,1)}, u32[]{:S(2)}) copy-start(bf16[1,64,1024]{2,1,0:T(8,128)(2,1)} %param.27) | copy-start | bytes 393220
  11.2 67.7 %all-to-all-start = ((bf16[16,1,64,1024]{3,2,1,0:T(8,128)(2,1)}), bf16[16,1,64,1024]{3,2,1,0:T(8,128)(2,1)S(1)}, u32[]{:S(2)}, u32[]{:S(2)}) async-start(bf16[16,1,64,1024]{3,2,1,0:T(8,128)(2,1)} %stack.2), calls=%async_computation | async-start | bytes 4194304 | tf_op jit(solution)/shard_map/all_to_all | solution.py:216
  19.9 242.5 %all-gather.8.cloned.1.call-start = ((), (), s32[]{:S(2)}) async-start(), calls=%async_computation.6 | async-start | bytes 4456448 | tf_op jit(solution)/shard_map/all_gather | solution.py:220
  20.7 451.6 %reduce-scatter.3.cloned.1.call-start = ((), (), s32[]{:S(2)}) async-start(), calls=%async_computation.4 | async-start | bytes 4456448 | tf_op jit(solution)/shard_map/reduce_scatter | solution.py:248
  22.9 60.0 %copy-start.7 = (bf16[1,64,1024]{1,2,0:T(8,128)(2,1)}, bf16[1,64,1024]{1,2,0:T(8,128)(2,1)S(1)}, u32[]{:S(2)}) copy-start(bf16[1,64,1024]{1,2,0:T(8,128)(2,1)S(1)} %copy.107) | copy-start | bytes 393220
  82.9 5.5 %copy-start.12 = (f32[32,16]{0,1:T(8,128)S(1)}, f32[32,16]{0,1:T(8,128)}, u32[]{:S(2)}) copy-start(f32[32,16]{0,1:T(8,128)} %param.33) | copy-start | bytes 6148
  96.9 1.6 slice-start
  112.9 1.6 slice-start
  133.0 1.6 slice-start.1
  134.6 2.5 copy-start.15
  140.5 0.8 copy-start.16
  150.0 1.6 slice-start.1
  151.6 2.5 copy-start.15
  157.5 0.8 copy-start.16
  159.6 12.8 %copy-start.9 = (bf16[64,16,64]{0,2,1:T(8,128)(2,1)}, bf16[64,16,64]{0,2,1:T(8,128)(2,1)S(1)}, u32[]{:S(2)}) copy-start(bf16[64,16,64]{0,2,1:T(8,128)(2,1)S(1)} %get-tuple-element.2055) | copy-start | bytes 393220 | tf_op jit(solution)/shard_map/while
  168.3 1.6 slice-start.2
  175.1 1.6 copy-start.2
  176.7 1.6 copy-start
  176.7 1.7 copy-start.3
  178.9 0.8 copy-start.4
  196.7 3.3 copy-start.10
  200.0 12.7 %copy-start.9 = (bf16[64,16,64]{0,2,1:T(8,128)(2,1)}, bf16[64,16,64]{0,2,1:T(8,128)(2,1)S(1)}, u32[]{:S(2)}) copy-start(bf16[64,16,64]{0,2,1:T(8,128)(2,1)S(1)} %get-tuple-element.2055) | copy-start | bytes 393220 | tf_op jit(solution)/shard_map/while
  208.6 1.6 slice-start.2
  215.4 1.6 copy-start.2
  217.0 1.6 copy-start
  217.0 1.7 copy-start.3
  219.2 0.8 copy-start.4
  237.0 3.3 copy-start.10
  240.3 6.9 %copy-start.11 = (bf16[64,16,64]{2,0,1:T(8,128)(2,1)S(1)}, bf16[64,16,64]{2,0,1:T(8,128)(2,1)}, u32[]{:S(2)}) copy-start(bf16[64,16,64]{2,0,1:T(8,128)(2,1)} %copy.108) | copy-start | bytes 393220
  240.3 6.9 %copy-start.13 = (f32[16,64]{1,0:T(8,128)S(1)}, f32[16,64]{1,0:T(8,128)}, u32[]{:S(2)}) copy-start(f32[16,64]{1,0:T(8,128)} %custom-call.5) | copy-start | bytes 12292
  240.3 6.9 %copy-start.17 = (f32[16,64]{1,0:T(8,128)S(1)}, f32[16,64]{1,0:T(8,128)}, u32[]{:S(2)}) copy-start(f32[16,64]{1,0:T(8,128)} %custom-call.6) | copy-start | bytes 12292
  240.3 6.9 %copy-start.18 = (s32[2048]{0:T(1024)S(1)}, s32[2048]{0:T(1024)}, u32[]{:S(2)}) copy-start(s32[2048]{0:T(1024)} %convert_reduce_fusion) | copy-start | bytes 24580
  240.3 233.6 %reduce-scatter.5.cloned.1.call-start = ((), (), s32[]{:S(2)}) async-start(), calls=%async_computation.7 | async-start | bytes 8912896 | tf_op jit(solution)/shard_map/reduce_scatter | solution.py:251
  262.4 6.7 %copy-start.14 = (f32[64,16,64]{0,2,1:T(8,128)S(1)}, f32[64,16,64]{0,2,1:T(8,128)}, u32[]{:S(2)}) copy-start(f32[64,16,64]{0,2,1:T(8,128)} %custom-call.7) | copy-start | bytes 786436
  269.1 16.1 %copy-start.1 = (bf16[1,64,1024]{1,2,0:T(8,128)(2,1)S(1)}, bf16[1,64,1024]{1,2,0:T(8,128)(2,1)}, u32[]{:S(2)}) copy-start(bf16[1,64,1024]{1,2,0:T(8,128)(2,1)} %copy.110) | copy-start | bytes 393220
  269.1 16.2 %copy-start.6 = (f32[64,16,64]{0,2,1:T(8,128)S(1)}, f32[64,16,64]{0,2,1:T(8,128)}, u32[]{:S(2)}) copy-start(f32[64,16,64]{0,2,1:T(8,128)} %custom-call.8) | copy-start | bytes 786436
  269.1 16.2 %copy-start.8 = (bf16[1,64,1024]{1,2,0:T(8,128)(2,1)S(1)}, bf16[1,64,1024]{1,2,0:T(8,128)(2,1)}, u32[]{:S(2)}) copy-start(bf16[1,64,1024]{1,2,0:T(8,128)(2,1)} %copy-done.7) | copy-start | bytes 393220
  339.4 1.0 copy-start.5
Sparse Core Ops, SparseCore 0:
  9.8 63.6 all-gather.3
  75.3 47.8 all-gather.5
  125.0 40.6 all-gather.7
  240.4 61.9 reduce-scatter.2
  339.5 70.3 reduce-scatter.4
